TPU v7x, 256 devices: a whole 4x4x8 slice. The times are simulated.
256 devices in a mesh: layer: 8 (over z_lo, y), cell: 32 (over z_hi, x, core).
Axes of the slice: x: 4, y: 4, z: 8 (z_hi: 4, z_lo: 2; z = z_hi * 2 + z_lo), core: 2. Of those that a mesh axis runs over, the one named last changes fastest.
Arguments:
- shower_state: float32 [2, 48, 1024], P(None, 'layer', 'cell'), may hold values from -6 to 6
- cell_valid: int32 [1024], replicated, may hold values 0 or 1
- layer_valid: int32 [48], replicated, may hold values 0 or 1
- energy_bin: int32 [2], replicated, may hold values from 0 to 63
- time_index: int32 [1], replicated, may hold values from 0 to 999
- embed_weight: float32 [512], replicated, may hold values from -6 to 6
- cell_embed: float32 [1024, 512], P('cell'), may hold values from -6 to 6
- layer_embed: float32 [48, 512], P('layer'), may hold values from -6 to 6
- energy_table: float32 [64, 512], replicated, may hold values from -6 to 6
- gain_cells: float32 [512], replicated, may hold values from 0.1 to 1.9
- cell_heads: bfloat16 [512, 1536], replicated, may hold values from -0.25 to 0.25
- cell_merge: bfloat16 [512, 512], replicated, may hold values from -0.25 to 0.25
- cell_scale: float32 [8], replicated, may hold values from 0.5 to 40
- gain_layers: float32 [512], replicated, may hold values from 0.1 to 1.9
- layer_heads: bfloat16 [512, 1536], replicated, may hold values from -0.25 to 0.25
- layer_merge: bfloat16 [512, 512], replicated, may hold values from -0.25 to 0.25
- layer_scale: float32 [8], replicated, may hold values from 0.5 to 40
- gain_expand: float32 [512], replicated, may hold values from 0.1 to 1.9
- expand_weight: bfloat16 [512, 2048], replicated, may hold values from -0.25 to 0.25
- reduce_weight: bfloat16 [2048, 512], replicated, may hold values from -0.125 to 0.125
- gain_final: float32 [512], replicated, may hold values from 0.1 to 1.9
- velocity_head: float32 [512], replicated, may hold values from -0.25 to 0.25
Outputs:
- velocity: float32 [2, 48, 1024], P(None, 'layer', 'cell')
- next_state: float32 [2, 48, 1024], P(None, 'layer', 'cell')
All inputs are finite; a program needn't handle non-finite values.
Results may differ from a plain program's by a relative error of at most 0.018.
The roundings to bfloat16 on the way count: a program that leaves them out, or rounds other values in their place, can miss the bound.
Values may be sent and summed in bfloat16 or wider, within the bound.
A program may use at most 192 MiB of HBM per device.

v0:
```python
import math

import jax
import jax.numpy as jnp
from jax import lax
from jax.sharding import PartitionSpec as P

D = 512
HEADS = 8
HDIM = 64
NBINS = 64
GRID = 1000
STEPS = 2


EPS = 1e-06


def normalize(hidden, gain):
    return hidden * lax.rsqrt(jnp.mean(hidden * hidden, -1, keepdims=True) + EPS) * gain


def head_norm(values):
    split = values.reshape(values.shape[:-1] + (HEADS, HDIM))
    return split * lax.rsqrt(jnp.mean(split * split, -1, keepdims=True) + EPS)


def split_heads(values):
    return values.reshape(values.shape[:-1] + (HEADS, HDIM)).astype(jnp.bfloat16)


def condition(energy_bin, time_index, energy_table):
    onehot = (jnp.arange(NBINS)[None, :] == energy_bin[:, None])[:, :, None]
    picked = jnp.sum(jnp.where(onehot, energy_table[None], 0.0), 1)
    moment = time_index[0].astype(jnp.float32) / GRID
    freqs = jnp.exp(-math.log(1000.0) * jnp.arange(D // 2).astype(jnp.float32) / (D // 2))
    angles = moment * 100.0 * freqs
    return picked + jnp.concatenate([jnp.sin(angles), jnp.cos(angles)])[None]


def online(carry, scores, allowed, values, form):
    top, total, accum = carry
    scores = jnp.where(allowed, scores, -1e30)
    new_top = jnp.maximum(top, jnp.max(scores, -1))
    weights = jnp.where(allowed, jnp.exp(scores - new_top[..., None]), 0.0)
    total = jnp.sum(weights, -1)
    accum = jnp.einsum(
        form, weights.astype(jnp.bfloat16), values, preferred_element_type=jnp.float32
    )
    return (new_top, total, accum)


def on_device(
    shower_state,
    cell_valid,
    layer_valid,
    energy_bin,
    time_index,
    embed_weight,
    cell_embed,
    layer_embed,
    energy_table,
    gain_cells,
    cell_heads,
    cell_merge,
    cell_scale,
    gain_layers,
    layer_heads,
    layer_merge,
    layer_scale,
    gain_expand,
    expand_weight,
    reduce_weight,
    gain_final,
    velocity_head,
):
    shw_count, lay_count, cell_count = shower_state.shape
    width = embed_weight.shape[0]
    cell_first = lax.axis_index("cell") * cell_count
    layer_first = lax.axis_index("layer") * lay_count
    cell_ok = lax.dynamic_slice_in_dim(cell_valid, cell_first, cell_count) == 1
    layer_ok = lax.dynamic_slice_in_dim(layer_valid, layer_first, lay_count) == 1
    cond = condition(energy_bin, time_index, energy_table)
    hidden = (
        shower_state[..., None] * embed_weight
        + cell_embed[None, None]
        + layer_embed[None, :, None]
        + cond[:, None, None]
    )
    normed = normalize(hidden, gain_cells).astype(jnp.bfloat16)
    query_ids = cell_first + jnp.arange(cell_count)
    cell_factor = cell_scale / math.sqrt(HDIM)
    start_cells = (
        jnp.full((shw_count, lay_count, HEADS, cell_count), -1e30, jnp.float32),
        jnp.zeros((shw_count, lay_count, HEADS, cell_count), jnp.float32),
        jnp.zeros((shw_count, lay_count, HEADS, cell_count, HDIM), jnp.float32),
    )
    queries = head_norm(
        jnp.dot(normed, cell_heads[:, :width], preferred_element_type=jnp.float32)
    ).astype(jnp.bfloat16)
    proj = jnp.dot(
        lax.all_gather(normed, "cell", axis=2, tiled=True),
        cell_heads[:, width:],
        preferred_element_type=jnp.float32,
    )
    keys = head_norm(proj[..., :width]).astype(jnp.bfloat16)
    values = split_heads(proj[..., width:])
    count = keys.shape[2]
    scores = (
        jnp.einsum("slqhd,slkhd->slhqk", queries, keys, preferred_element_type=jnp.float32)
        * cell_factor[None, None, :, None, None]
    )
    key_ok = cell_valid == 1
    allowed = key_ok[None, :] | (jnp.arange(count)[None, :] == query_ids[:, None])
    carry = online(start_cells, scores, allowed[None, None, None], values, "slhqk,slkhd->slhqd")
    result = carry[2] / carry[1][..., None]
    mixed = (
        jnp.transpose(result, (0, 1, 3, 2, 4))
        .reshape(shw_count, lay_count, cell_count, width)
        .astype(jnp.bfloat16)
    )
    hidden = hidden + jnp.dot(mixed, cell_merge, preferred_element_type=jnp.float32)
    normed = normalize(hidden, gain_layers).astype(jnp.bfloat16)
    layer_factor = layer_scale / math.sqrt(HDIM)
    proj = jnp.dot(normed, layer_heads, preferred_element_type=jnp.float32)
    layer_queries = head_norm(proj[..., :width]).astype(jnp.bfloat16)
    layer_keys = head_norm(proj[..., width : 2 * width]).astype(jnp.bfloat16)
    layer_values = split_heads(proj[..., 2 * width :])
    layer_ids = layer_first + jnp.arange(lay_count)
    start_layers = (
        jnp.full((shw_count, cell_count, HEADS, lay_count), -1e30, jnp.float32),
        jnp.zeros((shw_count, cell_count, HEADS, lay_count), jnp.float32),
        jnp.zeros((shw_count, cell_count, HEADS, lay_count, HDIM), jnp.float32),
    )
    pieces = (
        lax.all_gather(layer_keys, "layer", axis=1, tiled=True),
        lax.all_gather(layer_values, "layer", axis=1, tiled=True),
    )
    count = pieces[0].shape[1]
    scores = (
        jnp.einsum(
            "sqchd,skchd->schqk", layer_queries, pieces[0], preferred_element_type=jnp.float32
        )
        * layer_factor[None, None, :, None, None]
    )
    key_ok = layer_valid == 1
    allowed = key_ok[None, :] | (jnp.arange(count)[None, :] == layer_ids[:, None])
    carry = online(start_layers, scores, allowed[None, None, None], pieces[1], "schqk,skchd->schqd")
    result = carry[2] / carry[1][..., None]
    mixed = (
        jnp.transpose(result, (0, 3, 1, 2, 4))
        .reshape(shw_count, lay_count, cell_count, width)
        .astype(jnp.bfloat16)
    )
    hidden = hidden + jnp.dot(mixed, layer_merge, preferred_element_type=jnp.float32)
    normed = normalize(hidden, gain_expand).astype(jnp.bfloat16)
    inner = jax.nn.gelu(jnp.dot(normed, expand_weight, preferred_element_type=jnp.float32)).astype(
        jnp.bfloat16
    )
    hidden = hidden + jnp.dot(inner, reduce_weight, preferred_element_type=jnp.float32)
    velocity = jnp.sum(normalize(hidden, gain_final) * velocity_head, -1)
    velocity = (
        velocity
        * cell_ok[None, None, :].astype(jnp.float32)
        * layer_ok[None, :, None].astype(jnp.float32)
    )
    return (velocity, shower_state + velocity / STEPS)


def solution(mesh):
    return jax.shard_map(
        on_device,
        mesh=mesh,
        in_specs=(
            P(None, "layer", "cell"),
            P(),
            P(),
            P(),
            P(),
            P(),
            P("cell", None),
            P("layer", None),
            P(),
            P(),
            P(),
            P(),
            P(),
            P(),
            P(),
            P(),
            P(),
            P(),
            P(),
            P(),
            P(),
            P(),
        ),
        out_specs=(P(None, "layer", "cell"), P(None, "layer", "cell")),
        check_vma=False,
    )
```

profile of v0, /device:TPU:3, one launch (start us, length us, event | category | flops | bytes accessed | tf_op | source)
XLA Modules:
  0.0 405.9 jit_solution(17449303647220259367)
XLA Ops:
  7.2 0.0 copy-start
  7.2 0.0 all-gather.4.cloned.1.call-start
  7.2 0.9 iota_compare_fusion.2
  8.8 0.7 copy.68
  9.5 1.0 select_reduce_fusion
  10.5 1.1 multiply_reduce_fusion.8
  11.7 1.9 multiply_convert_fusion.8
  13.6 0.0 all-gather.4.cloned.1.call-update
  13.6 0.0 all-gather.6.cloned.1.call-start
  13.7 1.6 fusion.57
  15.3 1.5 reshape.228
  16.7 1.9 multiply_reduce_fusion.3
  18.6 0.1 copy.69
  18.8 0.1 copy.70
  18.9 0.1 fusion.66
  19.0 1.9 multiply_convert_fusion.3
  20.9 95.0 %all-gather.4.cloned.1.call-done = bf16[2,6,1024,512]{3,2,1,0:T(8,128)(2,1)} async-done(((bf16[2,6,32,512]{3,2,1,0:T(8,128)(2,1)}), bf16[2,6,1024,512]{3,2,1,0:T(8,128)(2,1)}) %all-gather.4.cloned.1.call-update) | async-done | bytes 12582928 | tf_op jit(solution)/shard_map/all_gather | solution.py:102
  115.9 24.7 %fusion.43 = f32[2,6,1024,1024]{2,3,1,0:T(8,128)} fusion(bf16[2,6,1024,512]{3,2,1,0:T(8,128)(2,1)} %all-gather.4.cloned.1.call-done, bf16[512,1536]{1,0:T(8,128)(2,1)} %param.32), kind=kOutput, calls=%fused_computation.53 | convolution fusion | flops 12884901888 | bytes 63963136 | tf_op jit(solution)/shard_map/dot_general | solution.py:101
  140.6 13.4 %slice.46 = bf16[2,6,1024,512]{2,3,1,0:T(8,128)(2,1)} slice(f32[2,6,1024,1024]{2,3,1,0:T(8,128)} %fusion.43), slice={[0:2], [0:6], [0:1024], [512:1024]} | slice | bytes 25165824 | tf_op jit(solution)/shard_map/slice | solution.py:107
  153.9 17.5 %slice.30 = f32[2,6,1024,512]{2,3,1,0:T(8,128)} slice(f32[2,6,1024,1024]{2,3,1,0:T(8,128)} %fusion.43), slice={[0:2], [0:6], [0:1024], [0:512]} | slice | bytes 50331648 | tf_op jit(solution)/shard_map/slice | solution.py:106
  171.5 10.2 %multiply_reduce_fusion = f32[2,6,1024,8]{2,3,1,0:T(8,128)S(1)} fusion(f32[2,6,1024,1024]{2,3,1,0:T(8,128)} %fusion.43), kind=kLoop, calls=%fused_computation.2 | loop fusion | flops 12484608 | bytes 25559040 | tf_op jit(solution)/shard_map/reduce_sum | solution.py:25
  181.7 0.1 add_rsqrt_fusion
  181.8 16.4 %fusion.2 = (f32[2,6,8,32]{3,2,1,0:T(8,128)S(1)}, f32[2,6,8,32,1024]{4,3,2,1,0:T(8,128)}) fusion(f32[8]{0:T(128)S(1)} %broadcast_multiply_fusion.1, pred[32,1024]{1,0:T(8,128)(4,1)S(1)} %fusion.66, f32[2,6,1024,8,64]{2,4,3,1,0:T(8,128)} %bitcast.78, f32[2,6,1024,8]{2,3,1,0:T(8,128)S(1)} %add_rsqrt_fusion, ...), kind=kOutput, calls=%fused_computation.7 | convolution fusion | flops 424670208 | bytes 38580256 | tf_op jit(solution)/shard_map/slqhd,slkhd->slhqk/dot_general | solution.py:110
  198.2 6.8 %fusion.3 = f32[2,6,8,32]{3,2,1,0:T(8,128)S(1)} fusion(f32[2,6,8,32,1024]{4,3,2,1,0:T(8,128)} %get-tuple-element.13, f32[2,6,8,32]{3,2,1,0:T(8,128)S(1)} %broadcast_maximum_fusion.1, f32[8]{0:T(128)S(1)} %broadcast_multiply_fusion.1, pred[32,1024]{1,0:T(8,128)(4,1)S(1)} %fusion.66), kind=kLoop, calls=%fused_computation.8 | loop fusion | flops 15725568 | bytes 12640288 | tf_op jit(solution)/shard_map/reduce_sum | solution.py:46
  205.0 14.3 %fusion.33 = bf16[2,6,32,8,64]{4,2,3,1,0:T(8,128)(2,1)} fusion(bf16[2,6,1024,8,64]{2,4,3,1,0:T(8,128)(2,1)} %bitcast.79, f32[2,6,8,32,1024]{4,3,2,1,0:T(8,128)} %get-tuple-element.13, f32[2,6,8,32]{3,2,1,0:T(8,128)S(1)} %broadcast_maximum_fusion.1, f32[8]{0:T(128)S(1)} %broadcast_multiply_fusion.1, pred[32,1024]{1,0:T(8,128)(4,1)S(1)} %fusion.66, ...), kind=kOutput, calls=%fused_computation.40 | convolution fusion | flops 418775040 | bytes 25616416 | tf_op jit(solution)/shard_map/slhqk,slkhd->slhqd/dot_general | solution.py:47
  219.3 1.5 copy.73
  220.7 0.5 convert_element_type.73
  221.3 1.6 multiply_reduce_fusion.7
  222.9 0.8 fusion.31
  223.8 1.4 copy-done.2
  225.2 1.0 fusion.78
  226.2 1.5 reshape.231
  227.7 1.9 multiply_reduce_fusion.1
  229.6 0.1 copy.76
  229.7 0.1 copy.77
  229.8 2.8 fusion.34
  232.6 0.0 all-gather.6.cloned.1.call-update
  232.6 0.0 all-gather.8.cloned.1.call-start
  232.7 1.2 slice.47
  233.9 0.4 convert_element_type.78
  234.3 1.0 copy.81
  235.2 0.0 all-gather.8.cloned.1.call-update
  235.3 0.1 compare_convert_fusion.1
  235.4 0.1 compare_convert_fusion
  235.4 0.1 fusion.67
  235.5 2.6 reshape.230
  238.1 1.9 multiply_reduce_fusion.2
  240.0 0.1 copy.74
  240.1 0.1 copy.75
  240.3 1.9 multiply_convert_fusion.2
  242.1 63.5 %all-gather.6.cloned.1.call-done = bf16[2,48,32,8,64]{4,3,2,0,1:T(8,128)(2,1)} async-done(((bf16[2,6,32,8,64]{4,3,2,0,1:T(8,128)(2,1)}), bf16[2,48,32,8,64]{4,3,2,0,1:T(8,128)(2,1)}) %all-gather.6.cloned.1.call-update) | async-done | bytes 3145744 | tf_op jit(solution)/shard_map/all_gather | solution.py:136
  305.7 8.8 %fusion.28 = (f32[2,32,8,6]{3,2,1,0:T(8,128)S(1)}, f32[2,32,8,6,48]{4,3,2,1,0:T(8,128)S(1)}) fusion(f32[8]{0:T(128)S(1)} %broadcast_multiply_fusion, pred[6,48]{1,0:T(8,128)(4,1)S(1)} %fusion.67, bf16[2,48,32,8,64]{4,3,2,0,1:T(8,128)(2,1)} %all-gather.6.cloned.1.call-done, bf16[2,6,32,8,64]{4,3,2,1,0:T(8,128)(2,1)S(1)} %multiply_convert_fusion.2), kind=kOutput, calls=%fused_computation.36 | convolution fusion | flops 19313664 | bytes 4141376 | tf_op jit(solution)/shard_map/sqchd,skchd->schqk/dot_general | solution.py:141
  314.4 1.3 copy-done.1
  315.8 1.5 fusion.37
  317.3 63.8 %all-gather.8.cloned.1.call-done = bf16[2,48,32,8,64]{4,3,2,0,1:T(8,128)(2,1)} async-done(((bf16[2,6,32,8,64]{4,3,2,0,1:T(8,128)(2,1)}), bf16[2,48,32,8,64]{4,3,2,0,1:T(8,128)(2,1)}) %all-gather.8.cloned.1.call-update) | async-done | bytes 3145744 | tf_op jit(solution)/shard_map/all_gather | solution.py:137
  381.1 8.7 %fusion.27 = bf16[2,6,32,8,64]{4,1,3,2,0:T(8,128)(2,1)S(1)} fusion(bf16[2,48,32,8,64]{4,3,2,0,1:T(8,128)(2,1)} %all-gather.8.cloned.1.call-done, f32[2,32,8,6,48]{4,3,2,1,0:T(8,128)} %copy-done.1, f32[2,6,32,8]{1,3,2,0:T(8,128)S(1)} %bitcast.80, f32[2,32,8,6]{3,2,1,0:T(8,128)S(1)} %broadcast_maximum_fusion, f32[8]{0:T(128)S(1)} %broadcast_multiply_fusion, ...), kind=kOutput, calls=%fused_computation.33 | convolution fusion | flops 20004864 | bytes 4153664 | tf_op jit(solution)/shard_map/schqk,skchd->schqd/dot_general | solution.py:47
  389.8 0.1 copy.83
  389.9 0.5 convert_element_type.80
  390.4 1.7 multiply_reduce_fusion.6
  392.2 4.5 %multiply_reduce_fusion.5 = (f32[2,6,32]{2,1,0:T(8,128)S(1)}, f32[2,6,32,512]{3,2,1,0:T(8,128)}) fusion(f32[2,6,32,512]{3,2,1,0:T(8,128)S(1)} %get-tuple-element.19, bf16[2048,512]{1,0:T(8,128)(2,1)S(1)} %copy-done, bf16[512,2048]{1,0:T(8,128)(2,1)} %param.40, f32[512]{0:T(512)S(1)} %copy-done.13, f32[2,6,32]{2,1,0:T(8,128)S(1)} %add_rsqrt_fusion.5), kind=kOutput, calls=%fused_computation.65 | convolution fusion | flops 1618869888 | bytes 5772288 | tf_op jit(solution)/shard_map/dot_general | solution.py:160
  396.7 1.4 multiply_reduce_fusion.4
  398.1 0.1 multiply_add_fusion
  398.2 0.6 copy.85
  398.8 0.6 copy.86
  (49 shorter events, 0.3 us)
Async XLA Ops:
  7.2 385.0 %copy-start = (bf16[2048,512]{1,0:T(8,128)(2,1)S(1)}, bf16[2048,512]{1,0:T(8,128)(2,1)}, u32[]{:S(2)}) copy-start(bf16[2048,512]{1,0:T(8,128)(2,1)} %param.41) | copy-start | bytes 6291460
  7.2 108.7 %all-gather.4.cloned.1.call-start = ((), (), s32[]{:S(2)}) async-start(), calls=%async_computation | async-start | bytes 12976128 | tf_op jit(solution)/shard_map/all_gather | solution.py:102
  13.6 292.1 %all-gather.6.cloned.1.call-start = ((), (), s32[]{:S(2)}) async-start(), calls=%async_computation.1 | async-start | bytes 7077888 | tf_op jit(solution)/shard_map/all_gather | solution.py:136
  13.6 5.3 %copy-start.14 = (f32[8]{0:T(128)S(1)}, f32[8]{0:T(128)}, u32[]{:S(2)}) copy-start(f32[8]{0:T(128)} %param.34) | copy-start | bytes 100
  13.7 5.3 %copy-start.10 = (s32[1024]{0:T(1024)S(1)}, s32[1024]{0:T(1024)}, u32[]{:S(2)}) copy-start(s32[1024]{0:T(1024)} %param.23) | copy-start | bytes 12292
  204.9 16.3 %copy-start.5 = (f32[32,512]{1,0:T(8,128)S(1)}, f32[32,512]{1,0:T(8,128)}, u32[]{:S(2)}) copy-start(f32[32,512]{1,0:T(8,128)} %param.28) | copy-start | bytes 196612
  204.9 16.3 %copy-start.6 = (f32[6,512]{1,0:T(8,128)S(1)}, f32[6,512]{1,0:T(8,128)}, u32[]{:S(2)}) copy-start(f32[6,512]{1,0:T(8,128)} %param.29) | copy-start | bytes 36868
  205.0 16.3 %copy-start.8 = (f32[512]{0:T(512)S(1)}, f32[512]{0:T(512)}, u32[]{:S(2)}) copy-start(f32[512]{0:T(512)} %param.27) | copy-start | bytes 6148
  219.3 3.6 copy-start.9
  221.2 1.7 copy-start.4
  222.9 3.3 copy-start.3
  223.8 1.4 copy-start.2
  232.6 2.8 copy-start.15
  232.6 2.8 copy-start.16
  232.6 148.5 %all-gather.8.cloned.1.call-start = ((), (), s32[]{:S(2)}) async-start(), calls=%async_computation.2 | async-start | bytes 7077888 | tf_op jit(solution)/shard_map/all_gather | solution.py:137
  314.4 1.4 copy-start.1
  389.8 2.4 copy-start.13
  392.2 4.6 %copy-start.11 = (f32[512]{0:T(512)S(1)}, f32[512]{0:T(512)}, u32[]{:S(2)}) copy-start(f32[512]{0:T(512)} %param.43) | copy-start | bytes 6148
  392.2 4.6 %copy-start.12 = (f32[512]{0:T(512)S(1)}, f32[512]{0:T(512)}, u32[]{:S(2)}) copy-start(f32[512]{0:T(512)} %param.42) | copy-start | bytes 6148
  392.2 5.9 %copy-start.7 = (f32[2,6,32]{2,0,1:T(2,128)S(1)}, f32[2,6,32]{2,0,1:T(2,128)}, u32[]{:S(2)}) copy-start(f32[2,6,32]{2,0,1:T(2,128)} %param.22) | copy-start | bytes 4612
Sparse Core Ops, SparseCore 0:
  13.7 102.1 all-gather.3
  232.8 72.8 all-gather.5
  307.4 73.6 all-gather.7
where the time goes:
time: 408 us; the launch traced here: 406 us
  waiting for transfers between devices  222 us (54%)
  matrix products  83.1 us (20%)
  local copies, waits for them, and re-layouts  47.8 us (12%)
  other arithmetic  37.7 us (9%)
  between operations  14.9 us (4%)
    all_gather x1, waiting for transfers between devices, on_device(): lax.all_gather(normed, 'cell', axis=2, tiled=True)  95 us
    all_gather x1, waiting for transfers between devices, on_device(): lax.all_gather(layer_values, 'layer', axis=1, tiled=True)  63.8 us
    all_gather x1, waiting for transfers between devices, on_device(): lax.all_gather(layer_keys, 'layer', axis=1, tiled=True)  63.5 us
    dot_general x1, matrix products, on_device(): jnp.dot(lax.all_gather(normed, 'cell', axis=2, tiled=True), cell_heads[:,...  24.7 us
    dot_general x2, matrix products, online(): jnp.einsum(form, weights.astype(jnp.bfloat16), values, preferred_element_...  23 us
    slice x1, local copies, waits for them, and re-layouts, on_device(): keys = head_norm(proj[..., :width]).astype(jnp.bfloat16)  17.5 us
    dot_general x1, matrix products, on_device(): jnp.einsum('slqhd,slkhd->slhqk', queries, keys, preferred_element_type=jn...  16.4 us
    reduce_sum x4, other arithmetic, head_norm(): return split * lax.rsqrt(jnp.mean(split * split, -1, keepdims=True) + EPS)  15.9 us
  transfers between devices with their start and end apart: 3, of which 3 were waited for; matrix products, arithmetic and copies ran while one was open for 7% of the time, Pallas kernels for 0%

commit v1 on v0

v1 whole, which is shorter than its diff:
```python
import functools
import math

import jax
import jax.numpy as jnp
from jax import lax
from jax.experimental import pallas as pl
from jax.experimental.pallas import tpu as pltpu
from jax.sharding import PartitionSpec as P

D = 512
HEADS = 8
HDIM = 64
NBINS = 64
GRID = 1000
STEPS = 2
EPS = 1e-06
LOG2E = math.log2(math.e)
F32 = jnp.float32
BF16 = jnp.bfloat16
MESH = pl.DeviceIdType.MESH
NT = (((1,), (1,)), ((), ()))


def iota(shape, axis):
    return lax.broadcasted_iota(jnp.int32, shape, axis)


def normed(hidden, gain):
    scale = lax.rsqrt(jnp.mean(hidden * hidden, -1, keepdims=True) + EPS)
    return (hidden * scale * gain).astype(BF16)


def head_norm_t(proj):
    parts = []
    for h in range(proj.shape[0] // HDIM):
        rows = proj[h * HDIM : (h + 1) * HDIM]
        scale = lax.rsqrt(jnp.mean(rows * rows, 0, keepdims=True) + EPS)
        parts.append(rows * scale)
    return parts


def kernel(
    bins,
    time,
    cell_scale,
    layer_scale,
    state,
    cell_valid,
    layer_valid,
    embed_w,
    cell_e,
    layer_e,
    table,
    gain1,
    gain2,
    gain3,
    gain4,
    vhead,
    heads1_h,
    merge1_h,
    heads2_h,
    merge2_h,
    expand_h,
    reduce_h,
    vel_out,
    next_out,
    heads1,
    merge1,
    heads2,
    merge2,
    expand,
    reduce,
    qkt1,
    qkt2,
    square,
    sx,
    ceb,
    leb,
    sdb,
    a1,
    kt,
    va,
    mask1,
    oacc,
    obuf,
    rbuf,
    o1,
    hid,
    vsend,
    vrecv,
    wsem,
    zs,
    zr,
    xs,
    xr,
    cs,
    cr,
    ls,
    lr,
    ss,
    sr,
    as_,
    ar,
    fs,
    fr,
):
    lam = lax.axis_index("layer")
    ci = lax.axis_index("cell")
    core = lax.rem(ci, 2)
    col = ci // 2
    x = lax.rem(col, 4)
    z = col // 4
    qb = col // 2
    b = lax.rem(col, 2)
    rank = lam * 2 + core

    z_dev = [(lam, (lax.rem(z + d, 4) * 4 + x) * 2 + core) for d in (1, 2, 3)]
    x_dev = [(lam, (z * 4 + lax.rem(x + d, 4)) * 2 + core) for d in (1, 3, 2)]
    sibling = (lam, col * 2 + 1 - core)
    quarter = lax.rem(ci, 4)
    holder = []
    for sb in range(2):
        for k in range(4):
            r = quarter * 4 + k
            holder.append((r // 2, (qb * 2 + sb) * 2 + lax.rem(r, 2)))
    owner = [(l, qb * 4 + rank // 4) for l in range(8)]

    def is_me(dev):
        return jnp.logical_and(dev[0] == lam, dev[1] == ci)

    barrier = pltpu.get_barrier_semaphore()

    def greet(dev):
        pl.semaphore_signal(barrier, inc=1, device_id=dev, device_id_type=MESH)

    for dev in z_dev + x_dev:
        greet(dev)
    for i in range(1, 16):
        r = lax.rem(rank + i, 16)
        greet((r // 2, col * 2 + lax.rem(r, 2)))
    for dev in holder + owner:

        @pl.when(jnp.logical_not(is_me(dev)))
        def _():
            greet(dev)

    selves = sum(jnp.where(is_me(dev), 1, 0) for dev in holder + owner)

    weights = [
        pltpu.make_async_copy(src, dst, wsem.at[i])
        for i, (src, dst) in enumerate(
            (
                (heads1_h, heads1),
                (merge1_h, merge1),
                (heads2_h, heads2),
                (merge2_h, merge2),
                (expand_h, expand),
                (reduce_h, reduce),
            )
        )
    ]
    for copy in weights:
        copy.start()

    square[...] = jnp.zeros_like(square)
    square[0:6, 0:32] = state[0]
    square[8:14, 0:32] = state[1]
    turned = jnp.transpose(square[...])[0:32]
    hit = iota((32, 1024), 1) == ci * 32 + iota((32, 1024), 0)
    own_ok = jnp.sum(jnp.where(hit, cell_valid[...].astype(F32), 0.0), -1, keepdims=True)
    lane = iota((32, 128), 1)
    sx[0] = turned
    sx[1] = pltpu.roll(turned, 120, 1)
    ceb[x, core, z, :, 0:D] = cell_e[...]
    ceb[x, core, z, :, D : D + 128] = jnp.where(lane == 16, own_ok, turned)
    leb[lam, 0:6, :] = layer_e[...]

    pl.semaphore_wait(barrier, 37 - selves)

    def push(src, dst, send, recv, dev):
        return pltpu.make_async_remote_copy(
            src_ref=src, dst_ref=dst, send_sem=send, recv_sem=recv, device_id=dev, device_id_type=MESH
        )

    z_out = []
    for i, dev in enumerate(z_dev):
        slot = ceb.at[x, core, z]
        z_out.append(push(slot, slot, zs.at[i], zr.at[i], dev))
        z_out[-1].start()

    for i, dev in enumerate(holder):
        src = sx.at[i // 4, pl.ds((i % 4) * 8, 8)]

        @pl.when(jnp.logical_not(is_me(dev)))
        def _():
            push(src, sdb.at[lam], ss.at[i], sr.at[lam], dev).start()

        @pl.when(is_me(dev))
        def _():
            sdb[lam] = sx[i // 4, (i % 4) * 8 : (i % 4) * 8 + 8]

    for i in range(1, 8):
        l = lax.rem(lam + i, 8)
        push(leb.at[lam], leb.at[lam], ls.at[i], lr.at[i], (l, ci)).start()

    picked = table[pl.ds(bins[b], 1), :]
    position = iota((1, D), 1)
    power = jnp.where(position < D // 2, position, position - D // 2).astype(F32)
    freqs = jnp.exp(-math.log(1000.0) * power / (D // 2))
    moment = jnp.full((1, D), time[0], jnp.int32).astype(F32) / GRID
    angles = moment * 100.0 * freqs
    cond = picked + jnp.where(position < D // 2, jnp.sin(angles), jnp.cos(angles))

    weights[0].wait()
    qkt1[...] = jnp.transpose(heads1[:, 0 : 2 * D])

    def block(l, chunk):
        rows = ceb[chunk].reshape(256, D + 128)
        lanes = pltpu.roll(rows[:, D:], lax.rem(128 - (b * 8 + core * 3 + l), 128), 1)
        hidden = lanes[:, 0:1] * embed_w[...] + rows[:, 0:D] + layer_e[pl.ds(core * 3 + l, 1), :] + cond
        act = normed(hidden, gain1[...])
        a1[l, chunk] = act.reshape(2, 4, 32, D)
        keys = lax.dot_general(qkt1[D : 2 * D], act, NT, preferred_element_type=F32)
        for h, part in enumerate(head_norm_t(keys)):
            kt[l, chunk, h * HDIM : (h + 1) * HDIM, :] = part.astype(BF16)
        va[l, chunk] = jnp.dot(act, heads1[:, 2 * D : 3 * D], preferred_element_type=F32).astype(BF16)

    def blocks(chunk):
        lax.fori_loop(0, 3, lambda l, _: (block(l, chunk), 0)[1], 0)

    for i, copy in enumerate(z_out):
        zz = lax.rem(z + 4 - (i + 1), 4)
        slot = ceb.at[x, core, zz]
        push(slot, slot, zs.at[i], zr.at[i], z_dev[i]).wait_recv()
    x_out = []
    for i, dev in enumerate(x_dev):
        slot = ceb.at[x, core]
        x_out.append(push(slot, slot, xs.at[i], xr.at[i], dev))
        x_out[-1].start()

    def to_sibling(n, chunk):
        mine = ceb.at[chunk, core]
        push(mine, mine, cs.at[n], cr.at[n], sibling).start()

    def from_sibling(n, chunk):
        theirs = ceb.at[chunk, 1 - core]
        push(theirs, theirs, cs.at[n], cr.at[n], sibling).wait_recv()

    to_sibling(0, x)
    from_sibling(0, x)
    blocks(x)
    chunks = [x] + [lax.rem(x + 4 - d, 4) for d in (1, 3, 2)]
    for n in (1, 2, 3):
        slot = ceb.at[chunks[n], core]
        push(slot, slot, xs.at[n - 1], xr.at[n - 1], x_dev[n - 1]).wait_recv()
        to_sibling(n, chunks[n])
        from_sibling(n, chunks[n])
        blocks(chunks[n])

    for c in range(4):
        side = jnp.transpose(ceb[c].reshape(256, D + 128)[:, D:])
        key_ok = side[16:17] > 0.5
        pos = iota((128, 256), 1)
        key = (lax.rem(pos // 32, 4) * 4 + c) * 64 + (pos // 128) * 32 + lax.rem(pos, 32)
        query = qb * 128 + iota((128, 256), 0)
        mask1[c] = jnp.where(jnp.logical_or(key_ok, key == query), 0.0, -1e30)

    pair = (x // 2) * 2

    def attend1(l, _):
        act = jnp.concatenate([a1[l, pair + i // 2, i % 2, z] for i in range(4)], 0)
        proj = lax.dot_general(qkt1[0:D], act, NT, preferred_element_type=F32)
        queries = head_norm_t(proj)
        for h in range(HEADS):
            query = jnp.transpose(queries[h]).astype(BF16)
            factor = cell_scale[h] * (LOG2E / math.sqrt(HDIM))
            scores = [
                jnp.dot(query, kt[l, c, h * HDIM : (h + 1) * HDIM, :], preferred_element_type=F32) + mask1[c]
                for c in range(4)
            ]
            top = jnp.maximum(jnp.maximum(scores[0], scores[1]), jnp.maximum(scores[2], scores[3]))
            top = jnp.max(top, -1, keepdims=True)
            total = jnp.zeros((128, 256), F32)
            mixed = jnp.zeros((128, 128), F32)
            first = (h // 2) * 128
            for c in range(4):
                p = jnp.exp2((scores[c] - top) * factor)
                total = total + p
                mixed = mixed + jnp.dot(
                    p.astype(BF16), va[l, c, :, first : first + 128], preferred_element_type=F32
                )
            mixed = mixed / jnp.sum(total, -1, keepdims=True)
            if h % 2 == 0:
                even = mixed
            else:
                oacc[l, :, first : first + 128] = jnp.where(iota((128, 128), 1) < HDIM, even, mixed)
        return 0

    lax.fori_loop(0, 3, attend1, 0)

    def fill(r, _):
        rows = pl.ds(pl.multiple_of(r * 8, 8), 8)
        obuf[r, :, 0:D] = jnp.concatenate([oacc[0, rows, :], oacc[1, rows, :]], 0).astype(BF16)
        last = oacc[2, rows, :]
        obuf[r, :, D : D + 256] = jnp.concatenate([last[:, 0:256], last[:, 256:D]], 0).astype(BF16)
        return 0

    lax.fori_loop(0, 16, fill, 0)
    for i in range(1, 16):
        r = lax.rem(rank + i, 16)
        push(obuf.at[r], rbuf.at[rank], as_.at[i], ar.at[i], (r // 2, col * 2 + lax.rem(r, 2))).start()
    rbuf[rank] = obuf[rank]

    weights[2].wait()
    qkt2[...] = jnp.transpose(heads2[:, 0 : 2 * D])
    for i in range(8):
        dev = owner[i]

        @pl.when(jnp.logical_not(is_me(dev)))
        def _():
            push(sx.at[0, pl.ds(0, 8)], sdb.at[i], ss.at[i], sr.at[i], dev).wait_recv()

    for i in range(1, 8):
        l = lax.rem(lam + 8 - i, 8)
        push(leb.at[l], leb.at[l], ls.at[i], lr.at[i], (l, ci)).wait_recv()

    eighth = lax.rem(rank, 4)
    ce8 = ceb[pair + rank // 8, lax.rem(rank // 4, 2), z, pl.ds(pl.multiple_of(eighth * 8, 8), 8), 0:D] + cond
    for l in range(48):
        column = sdb[l // 6][:, l % 6 : l % 6 + 1]
        hid[l * 8 : l * 8 + 8, :] = column * embed_w[...] + ce8 + leb[l // 6, l % 6 : l % 6 + 1, :]

    spread = (iota((48, 384), 1) // 8 == iota((48, 384), 0)).astype(BF16)
    layer_ok = jnp.dot(layer_valid[...].astype(F32).astype(BF16), spread, preferred_element_type=F32) > 0.5
    rows, cols = iota((384, 384), 0), iota((384, 384), 1)
    same = lax.rem(rows, 8) == lax.rem(cols, 8)
    allowed = jnp.logical_and(same, jnp.logical_or(layer_ok, rows == cols))
    mask2 = jnp.where(allowed, 0.0, -1e30)

    for i in range(1, 16):
        r = lax.rem(rank + 16 - i, 16)
        push(obuf.at[r], rbuf.at[r], as_.at[i], ar.at[i], (r // 2, col * 2 + lax.rem(r, 2))).wait_recv()

    for s in range(8):
        parts = []
        for i in (2 * s, 2 * s + 1):
            got = rbuf[i].astype(F32)
            parts += [got[:, 0:D], jnp.concatenate([got[0:8, D:], got[8:16, D:]], 1)]
        o1[48 * s : 48 * s + 48, :] = jnp.concatenate(parts, 0).astype(BF16)

    weights[1].wait()
    hidden = hid[...] + jnp.dot(o1[...], merge1[...], preferred_element_type=F32)
    hid[...] = hidden
    act = normed(hidden, gain2[...])
    proj = head_norm_t(lax.dot_general(qkt2[...], act, NT, preferred_element_type=F32))
    values = jnp.dot(act, heads2[:, 2 * D : 3 * D], preferred_element_type=F32).astype(BF16)
    for h in range(HEADS):
        query = jnp.transpose(proj[h]).astype(BF16)
        factor = layer_scale[h] * (LOG2E / math.sqrt(HDIM))
        scores = jnp.dot(query, proj[HEADS + h].astype(BF16), preferred_element_type=F32) + mask2
        top = jnp.max(scores, -1, keepdims=True)
        p = jnp.exp2((scores - top) * factor)
        first = (h // 2) * 128
        mixed = jnp.dot(p.astype(BF16), values[:, first : first + 128], preferred_element_type=F32)
        mixed = mixed / jnp.sum(p, -1, keepdims=True)
        if h % 2 == 0:
            even = mixed
        else:
            o1[:, first : first + 128] = jnp.where(iota((384, 128), 1) < HDIM, even, mixed).astype(BF16)

    weights[3].wait()
    hidden = hid[...] + jnp.dot(o1[...], merge2[...], preferred_element_type=F32)
    act = normed(hidden, gain3[...])
    weights[4].wait()
    weights[5].wait()
    for c in range(4):
        inner = jnp.dot(act, expand[:, c * 512 : c * 512 + 512], preferred_element_type=F32)
        inner = jax.nn.gelu(inner).astype(BF16)
        hidden = hidden + jnp.dot(inner, reduce[c * 512 : c * 512 + 512, :], preferred_element_type=F32)

    scale = lax.rsqrt(jnp.mean(hidden * hidden, -1, keepdims=True) + EPS)
    velocity = scale * jnp.sum(hidden * (gain4[...] * vhead[...]), -1, keepdims=True)
    lane = iota((8, 128), 1)
    tile = jnp.zeros((8, 128), F32)
    for l in range(48):
        tile = jnp.where(lane == l, velocity[l * 8 : l * 8 + 8], tile)
    first = qb * 128 + rank * 8
    hit = iota((8, 1024), 1) == first + iota((8, 1024), 0)
    cell_ok = jnp.sum(jnp.where(hit, cell_valid[...].astype(F32), 0.0), -1, keepdims=True)
    tile = tile * cell_ok
    for l in range(8):
        vsend[l] = tile if l == 0 else pltpu.roll(tile, 128 - 6 * l, 1)

    slot = b * 4 + eighth
    for l in range(8):
        dev = owner[l]

        @pl.when(jnp.logical_not(is_me(dev)))
        def _():
            push(vsend.at[l], vrecv.at[slot], fs.at[l], fr.at[slot], dev).start()

        @pl.when(is_me(dev))
        def _():
            vrecv[slot] = vsend[l]

    for i, dev in enumerate(holder):

        @pl.when(jnp.logical_not(is_me(dev)))
        def _():
            push(vsend.at[0], vrecv.at[i], fs.at[0], fr.at[i], dev).wait_recv()

    own = layer_valid[...]
    hit = iota((8, 48), 1) == lam * 6 + iota((8, 48), 0)
    own_layer = jnp.sum(jnp.where(hit, own.astype(F32), 0.0), -1, keepdims=True)[0:6]
    for sb in range(2):
        square[0:32, :] = vrecv[4 * sb : 4 * sb + 4].reshape(32, 128)
        vel = jnp.transpose(square[...])[0:6, 0:32] * own_layer
        vel_out[sb] = vel
        next_out[sb] = state[sb] + vel / STEPS

    for copy in z_out + x_out:
        copy.wait_send()
    for n in range(4):
        mine = ceb.at[chunks[n], core]
        push(mine, mine, cs.at[n], cr.at[n], sibling).wait_send()
    for i, dev in enumerate(holder):

        @pl.when(jnp.logical_not(is_me(dev)))
        def _():
            push(sx.at[0, pl.ds(0, 8)], sdb.at[lam], ss.at[i], sr.at[lam], dev).wait_send()

    for i in range(1, 8):
        push(leb.at[lam], leb.at[lam], ls.at[i], lr.at[i], (lax.rem(lam + i, 8), ci)).wait_send()
    for i in range(1, 16):
        r = lax.rem(rank + i, 16)
        push(obuf.at[r], rbuf.at[rank], as_.at[i], ar.at[i], (r // 2, col * 2 + lax.rem(r, 2))).wait_send()
    for l in range(8):
        dev = owner[l]

        @pl.when(jnp.logical_not(is_me(dev)))
        def _():
            push(vsend.at[l], vrecv.at[slot], fs.at[l], fr.at[slot], dev).wait_send()


def on_device(
    shower_state,
    cell_valid,
    layer_valid,
    energy_bin,
    time_index,
    embed_weight,
    cell_embed,
    layer_embed,
    energy_table,
    gain_cells,
    cell_heads,
    cell_merge,
    cell_scale,
    gain_layers,
    layer_heads,
    layer_merge,
    layer_scale,
    gain_expand,
    expand_weight,
    reduce_weight,
    gain_final,
    velocity_head,
):
    row = lambda v: v.reshape(1, -1)
    smem = pl.BlockSpec(memory_space=pltpu.SMEM)
    vmem = pl.BlockSpec(memory_space=pltpu.VMEM)
    hbm = pl.BlockSpec(memory_space=pl.ANY)
    dma = lambda n: pltpu.SemaphoreType.DMA((n,))
    shape = jax.ShapeDtypeStruct(shower_state.shape, F32)
    return pl.pallas_call(
        kernel,
        out_shape=(shape, shape),
        in_specs=[smem] * 4 + [vmem] * 12 + [hbm] * 6,
        out_specs=(vmem, vmem),
        scratch_shapes=[
            pltpu.VMEM((D, 3 * D), BF16),
            pltpu.VMEM((D, D), BF16),
            pltpu.VMEM((D, 3 * D), BF16),
            pltpu.VMEM((D, D), BF16),
            pltpu.VMEM((D, 4 * D), BF16),
            pltpu.VMEM((4 * D, D), BF16),
            pltpu.VMEM((2 * D, D), BF16),
            pltpu.VMEM((2 * D, D), BF16),
            pltpu.VMEM((128, 128), F32),
            pltpu.VMEM((2, 32, 128), F32),
            pltpu.VMEM((4, 2, 4, 32, D + 128), F32),
            pltpu.VMEM((8, 8, D), F32),
            pltpu.VMEM((8, 8, 128), F32),
            pltpu.VMEM((3, 4, 2, 4, 32, D), BF16),
            pltpu.VMEM((3, 4, D, 256), BF16),
            pltpu.VMEM((3, 4, 256, D), BF16),
            pltpu.VMEM((4, 128, 256), F32),
            pltpu.VMEM((3, 128, D), F32),
            pltpu.VMEM((16, 16, D + 256), BF16),
            pltpu.VMEM((16, 16, D + 256), BF16),
            pltpu.VMEM((384, D), BF16),
            pltpu.VMEM((384, D), F32),
            pltpu.VMEM((8, 8, 128), F32),
            pltpu.VMEM((8, 8, 128), F32),
        ]
        + [dma(n) for n in (6, 3, 3, 3, 3, 4, 4, 8, 8, 8, 8, 16, 16, 8, 8)],
        compiler_params=pltpu.CompilerParams(
            collective_id=0, has_side_effects=True, vmem_limit_bytes=56 * 1024 * 1024
        ),
    )(
        energy_bin,
        time_index,
        cell_scale,
        layer_scale,
        shower_state,
        row(cell_valid),
        row(layer_valid),
        row(embed_weight),
        cell_embed,
        layer_embed,
        energy_table,
        row(gain_cells),
        row(gain_layers),
        row(gain_expand),
        row(gain_final),
        row(velocity_head),
        cell_heads,
        cell_merge,
        layer_heads,
        layer_merge,
        expand_weight,
        reduce_weight,
    )


def solution(mesh):
    return jax.shard_map(
        on_device,
        mesh=mesh,
        in_specs=(
            P(None, "layer", "cell"),
            P(),
            P(),
            P(),
            P(),
            P(),
            P("cell", None),
            P("layer", None),
        )
        + (P(),) * 14,
        out_specs=(P(None, "layer", "cell"), P(None, "layer", "cell")),
        check_vma=False,
    )
```

time: 408 us -> 83.7 us (0.21)
  waiting for transfers between devices: 222 us -> 0 us
  matrix products: 83.1 us -> 0 us
  Pallas kernels: 0 us -> 78.3 us
  local copies, waits for them, and re-layouts: 47.8 us -> 3.87 us
  other arithmetic: 37.7 us -> 0 us
  between operations: 14.9 us -> 1.29 us
    all_gather x3 -> x0, waiting for transfers between devices: 222 us -> none  [the longest x1 95 us: on_device(): lax.all_gather(normed, 'cell', axis=2, tiled=True)]
    dot_general x10 -> x0, matrix products: 83.1 us -> none  [the longest x1 24.7 us: on_device(): jnp.dot(lax.all_gather(normed, 'cell', axis=2, tiled=True), cell_heads[:,...]
    pallas_call x0 -> x1, Pallas kernels: none -> 78.3 us  [on_device(): pl.pallas_call(kernel, out_shape=(shape, shape), in_specs=[smem] * 4 + [v...]
    slice x4 -> x0, local copies, waits for them, and re-layouts: 33.1 us -> none  [the longest x1 17.5 us: on_device(): keys = head_norm(proj[..., :width]).astype(jnp.bfloat16)]
    reduce_sum x9 -> x0, other arithmetic: 27.7 us -> none  [the longest x4 15.9 us: head_norm(): return split * lax.rsqrt(jnp.mean(split * split, -1, keepdims=True) + EPS)]
    convert_element_type x6 -> x0, other arithmetic: 8.57 us -> none  [the longest x1 2.79 us: on_device(): layer_keys = head_norm(proj[..., width:2 * width]).astype(jnp.bfloat16)]
    reshape x3 -> x0, local copies, waits for them, and re-layouts: 5.53 us -> none  [head_norm(): split = values.reshape(values.shape[:-1] + (HEADS, HDIM))]
  transfers between devices with their start and end apart: 3 -> 0, of which waited for: 3 -> 0; matrix products, arithmetic and copies ran while one was open for 7% -> 0% of each run, Pallas kernels for 0% -> 0%
where the time goes in v1:
time: 83.7 us; the launch traced here: 83.4 us
  Pallas kernels  78.3 us (94%)
  local copies, waits for them, and re-layouts  3.87 us (5%)
  between operations  1.29 us (2%)
    pallas_call x1, Pallas kernels, on_device(): pl.pallas_call(kernel, out_shape=(shape, shape), in_specs=[smem] * 4 + [v...  78.3 us
    pallas_call x2, local copies, waits for them, and re-layouts, on_device(): pl.pallas_call(kernel, out_shape=(shape, shape), in_specs=[smem] * 4 + [v...  2.59 us

profile of v1, /device:TPU:3, one launch (start us, length us, event | category | flops | bytes accessed | tf_op | source)
XLA Modules:
  0.0 83.4 jit_solution(13771719029282227858)
XLA Ops:
  1.3 1.3 %copy.24.state = f32[2,6,32]{2,1,0:T(8,128)} copy(f32[2,6,32]{2,0,1:T(2,128)} %param.22) | data formatting | bytes 3072 | tf_op args[0]
  2.6 78.3 %shard_map.221 = (f32[2,6,32]{2,1,0:T(8,128)}, f32[2,6,32]{2,1,0:T(8,128)}) custom-call(s32[2]{0:T(128)} %bins.1, s32[1]{0:T(128)S(6)} %copy.27.time, f32[8]{0:T(128)} %cell_scale.1, f32[8]{0:T(128)} %layer_scale.1, f32[2,6,32]{2,1,0:T(8,128)} %copy.24.state, s32[1,1024]{1,0:T(1,128)} %bitcast.8, s32[1,48]{1,0:T(1,128)} %bitcast.15, f32[1,512]{1,0:T(1,128)} %bitcast.9, ...), custom_call_target="tpu_custom_call" | custom-call | tf_op jit(solution)/shard_map/pallas_call | solution.py:476
  80.8 1.3 %copy.25 = f32[2,6,32]{2,0,1:T(2,128)} copy(f32[2,6,32]{2,1,0:T(8,128)} %get-tuple-element.2) | data formatting | bytes 3072 | tf_op jit(solution)/shard_map/pallas_call | solution.py:476
  82.1 1.3 %copy.26 = f32[2,6,32]{2,0,1:T(2,128)} copy(f32[2,6,32]{2,1,0:T(8,128)} %get-tuple-element.3) | data formatting | bytes 3072 | tf_op jit(solution)/shard_map/pallas_call | solution.py:476
